TPU v7x, 512 devices: a whole 4x4x16 slice. The times are simulated.
512 devices in a mesh: ctx: 8 (over x_hi, y), fsdp: 64 (over x_lo, z, core).
Axes of the slice: x: 4 (x_hi: 2, x_lo: 2; x = x_hi * 2 + x_lo), y: 4, z: 16, core: 2. Of those that a mesh axis runs over, the one named last changes fastest.
Arguments:
- hidden_rows: bfloat16 [64, 1024, 4608], P('fsdp', 'ctx'), may hold values from -6 to 6
- query_proj: bfloat16 [64, 1024, 2048], P('fsdp', 'ctx'), may hold values from -10 to 10
- key_proj: bfloat16 [64, 1024, 1024], P('fsdp', 'ctx'), may hold values from -10 to 10
- value_proj: bfloat16 [64, 1024, 1024], P('fsdp', 'ctx'), may hold values from -6 to 6
- order_pos: int32 [64, 1024], P('fsdp', 'ctx'), may hold values from 0 to 1023, each once within a row
- post_gain: float32 [4608], replicated, may hold values from 0.5 to 1.5
- out_weight: bfloat16 [2048, 4608], P('fsdp', 'ctx'), may hold values from -0.125 to 0.125
Outputs:
- residual_out: bfloat16 [64, 1024, 4608], P('fsdp', 'ctx')
Inputs may be any that keep to these rules, and one draw needn't show every extreme that they name: Each document's row of order_pos holds every position of 0 to 1023 exactly once.
All inputs are finite; a program needn't handle non-finite values.
Results may differ from a plain program's by a relative error of at most 0.0053.
Values may be sent and summed in bfloat16 or wider, within the bound.
A program may use at most 64 MiB of HBM per device.

v0:
```python
import jax
import jax.numpy as jnp
from jax import lax
from jax.sharding import PartitionSpec as P

HQ = 16
HK = 8
DH = 128
score_scale = 1.0 / 12.0
soft_cap = 50.0
norm_eps = 1e-06


def weigh_keys(query_heads, query_pos, key_heads, value_heads, key_pos):
    scores = (
        jnp.einsum("thgd,nhd->hgtn", query_heads, key_heads, preferred_element_type=jnp.float32)
        * score_scale
    )
    capped = soft_cap * jnp.tanh(scores / soft_cap)
    visible = key_pos[None, :] <= query_pos[:, None]
    weights = jnp.where(visible, jnp.exp(capped), 0.0)
    rounded = weights.astype(jnp.bfloat16)
    numerator = jnp.einsum(
        "hgtn,nhd->thgd", rounded, value_heads, preferred_element_type=jnp.float32
    )
    denominator = jnp.transpose(jnp.sum(weights, axis=-1), (2, 0, 1))
    return (numerator, denominator)


def shards(hidden_rows, query_proj, key_proj, value_proj, order_pos, post_gain, out_weight):
    tokens = query_proj.shape[1]
    groups = HQ // HK
    all_positions = lax.all_gather(order_pos, "ctx", axis=1, tiled=True)[0]
    weight_block = lax.all_gather(out_weight, "fsdp", axis=0, tiled=True)
    own_pos = order_pos[0]
    query_heads = query_proj[0].reshape(tokens, HK, groups, DH)
    key_piece = lax.all_gather(key_proj, "ctx", axis=1, tiled=True)
    value_piece = lax.all_gather(value_proj, "ctx", axis=1, tiled=True)
    piece_rows = key_piece.shape[1]
    numerator, denominator = weigh_keys(
        query_heads,
        own_pos,
        key_piece[0].reshape(piece_rows, HK, DH),
        value_piece[0].reshape(piece_rows, HK, DH),
        all_positions,
    )
    numerator, denominator = (numerator, denominator)
    attended = (numerator / denominator[..., None]).astype(jnp.bfloat16).reshape(1, tokens, HQ * DH)
    projected = jnp.dot(
        lax.all_gather(attended, "ctx", axis=1, tiled=True)[0],
        weight_block,
        preferred_element_type=jnp.float32,
    )
    token_rows = lax.all_to_all(
        projected.astype(jnp.bfloat16), "ctx", split_axis=0, concat_axis=1, tiled=True
    )
    widened = token_rows.astype(jnp.float32)
    normed = (
        widened
        * lax.rsqrt(jnp.mean(widened * widened, axis=-1, keepdims=True) + norm_eps)
        * post_gain
    )
    return (hidden_rows[0].astype(jnp.float32) + normed).astype(jnp.bfloat16)[None]


def solution(mesh):
    placed = (
        P("fsdp", "ctx", None),
        P("fsdp", "ctx", None),
        P("fsdp", "ctx", None),
        P("fsdp", "ctx", None),
        P("fsdp", "ctx"),
        P(),
        P("fsdp", "ctx"),
    )
    return jax.shard_map(
        shards, mesh=mesh, in_specs=placed, out_specs=P("fsdp", "ctx", None), check_vma=False
    )
```

profile of v0, /device:TPU:32, one launch (start us, length us, event | category | flops | bytes accessed | tf_op | source)
XLA Modules:
  0.0 404.5 jit_solution(9914539973454579862)
XLA Ops:
  6.5 0.7 all-gather.7.cloned.1.call-update
  7.3 1.8 copy.13
  9.1 0.0 all-gather.11.cloned.1.call-start
  9.2 0.7 all-gather.11.cloned.1.call-update
  9.9 0.0 all-gather.9.cloned.1.call-start
  9.9 1.4 reshape_squeeze.10
  11.3 23.6 %all_gather.15 = s32[1,1024]{1,0:T(1,128)S(1)} all-gather(s32[1,128]{1,0:T(1,128)} %param.11), channel_id=1, replica_groups=mesh['ctx'=8,'fsdp'=64] {'ctx'}, dimensions={1}, use_global_device_ids=true | all-gather | bytes 4608 | tf_op jit(solution)/shard_map/all_gather | solution.py:33
  34.9 0.9 broadcast_compare_fusion
  35.8 48.2 %all-gather.7.cloned.1.call-done = bf16[1,1024,1024]{2,1,0:T(8,128)(2,1)} async-done(((bf16[1,128,1024]{2,1,0:T(8,128)(2,1)}), bf16[1,1024,1024]{2,1,0:T(8,128)(2,1)}) %all-gather.7.cloned.1.call-update) | async-done | bytes 2097168 | tf_op jit(solution)/shard_map/all_gather | solution.py:38
  84.0 2.9 copy.16
  86.9 68.0 %all-gather.5.cloned.1.call-done = bf16[1,1024,1024]{1,2,0:T(8,128)(2,1)} async-done(((bf16[1,128,1024]{1,2,0:T(8,128)(2,1)}), bf16[1,1024,1024]{1,2,0:T(8,128)(2,1)}) %all-gather.5.cloned.1.call-update) | async-done | bytes 2097168 | tf_op jit(solution)/shard_map/all_gather | solution.py:37
  154.9 4.1 %fusion = (f32[8,2,128]{2,1,0:T(2,128)S(1)}, f32[8,1024,128,2]{2,1,3,0:T(8,128)S(1)}) fusion(pred[128,1024]{0,1:T(8,128)(4,1)S(1)} %broadcast_compare_fusion, bf16[1024,8,128,1]{0,2,3,1:T(8,128)(2,1)} %bitcast.60, bf16[128,8,2,128]{3,2,1,0:T(2,128)(2,1)S(1)} %reshape_squeeze.10), kind=kOutput, calls=%fused_computation.1 | convolution fusion | flops 545257472 | bytes 11149312 | tf_op jit(solution)/shard_map/thgd,nhd->hgtn/dot_general | solution.py:16
  159.0 3.4 divide_convert_fusion
  162.4 115.8 %all-gather.11.cloned.1.call-done = bf16[2048,576]{1,0:T(8,128)(2,1)} async-done(((bf16[32,576]{1,0:T(8,128)(2,1)}), bf16[2048,576]{1,0:T(8,128)(2,1)}) %all-gather.11.cloned.1.call-update) | async-done | bytes 2359312 | tf_op jit(solution)/shard_map/all_gather | solution.py:34
  278.3 88.1 %all-gather.9.cloned.1.call-done = bf16[1,1024,2048]{1,2,0:T(8,128)(2,1)} async-done(((bf16[1,128,2048]{1,2,0:T(8,128)(2,1)}), bf16[1,1024,2048]{1,2,0:T(8,128)(2,1)}) %all-gather.9.cloned.1.call-update) | async-done | bytes 4194320 | tf_op jit(solution)/shard_map/all_gather | solution.py:50
  366.4 5.7 %fusion.13 = bf16[72,8,8,128]{3,2,1,0:T(8,128)(2,1)S(1)} fusion(bf16[2048,576]{1,0:T(8,128)(2,1)} %all-gather.11.cloned.1.call-done, bf16[1,1024,2048]{1,2,0:T(8,128)(2,1)} %all-gather.9.cloned.1.call-done), kind=kOutput, calls=%fused_computation.13 | convolution fusion | flops 2416508928 | bytes 7733248 | tf_op jit(solution)/shard_map/dot_general | solution.py:49
  372.1 1.2 copy.31
  373.3 3.6 all-to-all-start
  376.9 0.7 copy.12
  377.7 16.1 %all-to-all-done = bf16[8,128,576]{1,2,0:T(8,128)(2,1)S(1)} async-done(((bf16[8,128,576]{1,2,0:T(8,128)(2,1)}), bf16[8,128,576]{1,2,0:T(8,128)(2,1)S(1)}, u32[]{:S(2)}, u32[]{:S(2)}) %all-to-all-start) | async-done | bytes 1179680 | tf_op jit(solution)/shard_map/all_to_all | solution.py:54
  393.8 0.6 multiply_reduce_fusion
  394.4 0.2 convert_element_type.47
  394.6 2.0 fusion.9
  396.6 1.4 copy.19
  (9 shorter events, 0.1 us)
Async XLA Ops:
  6.5 77.5 %all-gather.7.cloned.1.call-start = ((), (), s32[]{:S(2)}) async-start(), calls=%async_computation.2 | async-start | bytes 2359296 | tf_op jit(solution)/shard_map/all_gather | solution.py:38
  7.3 147.6 %all-gather.5.cloned.1.call-start = ((), (), s32[]{:S(2)}) async-start(), calls=%async_computation.1 | async-start | bytes 2359296 | tf_op jit(solution)/shard_map/all_gather | solution.py:37
  9.1 269.2 %all-gather.11.cloned.1.call-start = ((), (), s32[]{:S(2)}) async-start(), calls=%async_computation.4 | async-start | bytes 2662400 | tf_op jit(solution)/shard_map/all_gather | solution.py:34
  9.9 356.6 %all-gather.9.cloned.1.call-start = ((), (), s32[]{:S(2)}) async-start(), calls=%async_computation.3 | async-start | bytes 4718592 | tf_op jit(solution)/shard_map/all_gather | solution.py:50
  372.1 4.8 %copy-start = (bf16[1,128,4608]{2,1,0:T(8,128)(2,1)S(1)}, bf16[1,128,4608]{2,1,0:T(8,128)(2,1)}, u32[]{:S(2)}) copy-start(bf16[1,128,4608]{2,1,0:T(8,128)(2,1)} %param.7) | copy-start | bytes 3538948
  373.3 20.5 %all-to-all-start = ((bf16[8,128,576]{1,2,0:T(8,128)(2,1)}), bf16[8,128,576]{1,2,0:T(8,128)(2,1)S(1)}, u32[]{:S(2)}, u32[]{:S(2)}) async-start(bf16[8,128,576]{1,2,0:T(8,128)(2,1)} %bitcast.53), calls=%async_computation | async-start | bytes 2359296 | tf_op jit(solution)/shard_map/all_to_all | solution.py:54
  377.7 16.9 %copy-start.1 = (f32[4608]{0:T(1024)S(1)}, f32[4608]{0:T(1024)}, u32[]{:S(2)}) copy-start(f32[4608]{0:T(1024)} %param.12) | copy-start | bytes 55300
Sparse Core Ops, SparseCore 0:
  10.6 73.4 all-gather.6
  87.1 67.7 all-gather.4
  157.0 121.2 all-gather.10
  281.2 85.1 all-gather.8
where the time goes:
time: 405 us
  waiting for transfers between devices  338 us (83%)
  blocking collectives  23.6 us (6%)
  matrix products  13.2 us (3%)
  between operations  13.2 us (3%)
  local copies, waits for them, and re-layouts  9.43 us (2%)
    all_gather x1, waiting for transfers between devices, shards(): weight_block = lax.all_gather(out_weight, 'fsdp', axis=0, tiled=True)  116 us
    all_gather x1, waiting for transfers between devices, shards(): lax.all_gather(attended, 'ctx', axis=1, tiled=True)[0]  88.1 us
    all_gather x1, waiting for transfers between devices, shards(): key_piece = lax.all_gather(key_proj, 'ctx', axis=1, tiled=True)  68 us
    all_gather x1, waiting for transfers between devices, shards(): value_piece = lax.all_gather(value_proj, 'ctx', axis=1, tiled=True)  48.2 us
    all_gather x1, blocking collectives, shards(): all_positions = lax.all_gather(order_pos, 'ctx', axis=1, tiled=True)[0]  23.6 us
    all_to_all x1, waiting for transfers between devices, shards(): lax.all_to_all(projected.astype(jnp.bfloat16), 'ctx', split_axis=0, conca...  16.1 us
  transfers between devices with their start and end apart: 5, of which 5 were waited for; matrix products, arithmetic and copies ran while one was open for 4% of the time, Pallas kernels for 0%

commit v1 on v0

--- a/solution.py
+++ b/solution.py
@@ -35,7 +35,9 @@
     own_pos = order_pos[0]
     query_heads = query_proj[0].reshape(tokens, HK, groups, DH)
     key_piece = lax.all_gather(key_proj, "ctx", axis=1, tiled=True)
-    value_piece = lax.all_gather(value_proj, "ctx", axis=1, tiled=True)
+    value_piece = jnp.concatenate(
+        lax.all_to_all(jnp.stack([value_proj] * lax.axis_size("ctx")), "ctx", 0, 0), axis=1
+    )
     piece_rows = key_piece.shape[1]
     numerator, denominator = weigh_keys(
         query_heads,

time: 405 us -> 343 us (0.85)
  waiting for transfers between devices: 338 us -> 247 us
  blocking collectives: 23.6 us -> 42 us
  starting transfers between devices: 3.69 us -> 10.7 us
  local copies, waits for them, and re-layouts: 9.43 us -> 13.7 us
    all_gather x1 -> x0, waiting for transfers between devices: 48.2 us -> none  [shards(): value_piece = lax.all_gather(value_proj, 'ctx', axis=1, tiled=True)]
    all_gather x1, waiting for transfers between devices: 68 us -> 26.2 us  [shards(): key_piece = lax.all_gather(key_proj, 'ctx', axis=1, tiled=True)]
    all_gather x1, blocking collectives: 23.6 us -> 42 us  [shards(): all_positions = lax.all_gather(order_pos, 'ctx', axis=1, tiled=True)[0]]
    all_to_all x0 -> x1, starting transfers between devices: none -> 7.06 us  [shards(): lax.all_to_all(jnp.stack([value_proj] * lax.axis_size('ctx')), 'ctx', 0, 0)]
    another operation x0 -> x3, local copies, waits for them, and re-layouts: none -> 5.53 us  [the longest x1 2.82 us: shards(): value_piece[0].reshape(piece_rows, HK, DH)]
  transfers between devices with their start and end apart: 5 -> 5, of which waited for: 5 -> 4; matrix products, arithmetic and copies ran while one was open for 4% -> 5% of each run, Pallas kernels for 0% -> 0%
where the time goes in v1:
time: 343 us
  waiting for transfers between devices  247 us (72%)
  blocking collectives  42 us (12%)
  local copies, waits for them, and re-layouts  13.7 us (4%)
  matrix products  13.2 us (4%)
  between operations  13.2 us (4%)
  starting transfers between devices  10.7 us (3%)
    all_gather x1, waiting for transfers between devices, shards(): weight_block = lax.all_gather(out_weight, 'fsdp', axis=0, tiled=True)  116 us
    all_gather x1, waiting for transfers between devices, shards(): lax.all_gather(attended, 'ctx', axis=1, tiled=True)[0]  88.3 us
    all_gather x1, blocking collectives, shards(): all_positions = lax.all_gather(order_pos, 'ctx', axis=1, tiled=True)[0]  42 us
    all_gather x1, waiting for transfers between devices, shards(): key_piece = lax.all_gather(key_proj, 'ctx', axis=1, tiled=True)  26.2 us
    all_to_all x1, waiting for transfers between devices, shards(): lax.all_to_all(projected.astype(jnp.bfloat16), 'ctx', split_axis=0, conca...  16.1 us
    all_to_all x1, starting transfers between devices, shards(): lax.all_to_all(jnp.stack([value_proj] * lax.axis_size('ctx')), 'ctx', 0, 0)  7.06 us
  transfers between devices with their start and end apart: 5, of which 4 were waited for; matrix products, arithmetic and copies ran while one was open for 5% of the time, Pallas kernels for 0%

profile of v1, /device:TPU:32, one launch (start us, length us, event | category | flops | bytes accessed | tf_op | source)
XLA Modules:
  0.0 343.0 jit_solution(17960908994380285857)
XLA Ops:
  6.5 1.8 copy.21
  8.4 0.7 all-gather.8.cloned.1.call-update
  9.1 1.1 copy.24
  10.2 1.6 stack.2
  11.8 7.1 %all-to-all-start = ((bf16[8,1,128,1024]{2,3,1,0:T(8,128)(2,1)}), bf16[8,1,128,1024]{2,3,1,0:T(8,128)(2,1)S(1)}, u32[]{:S(2)}, u32[]{:S(2)}) async-start(bf16[8,1,128,1024]{2,3,1,0:T(8,128)(2,1)} %stack.2), calls=%async_computation | async-start | bytes 4194304 | tf_op jit(solution)/shard_map/all_to_all | solution.py:39
  18.9 0.4 reshape_squeeze.7
  19.3 42.0 %all_gather.12 = s32[1,1024]{1,0:T(1,128)S(1)} all-gather(s32[1,128]{1,0:T(1,128)S(1)} %copy-done.3), channel_id=1, replica_groups=mesh['ctx'=8,'fsdp'=64] {'ctx'}, dimensions={1}, use_global_device_ids=true | all-gather | bytes 4608 | tf_op jit(solution)/shard_map/all_gather | solution.py:33
  61.3 0.2 broadcast_compare_fusion
  61.5 2.7 copy.25
  64.2 2.8 reshape.81
  67.0 26.2 %all-gather.4.cloned.1.call-done = bf16[1,1024,1024]{1,2,0:T(8,128)(2,1)} async-done(((bf16[1,128,1024]{1,2,0:T(8,128)(2,1)}), bf16[1,1024,1024]{1,2,0:T(8,128)(2,1)}) %all-gather.4.cloned.1.call-update) | async-done | bytes 2097168 | tf_op jit(solution)/shard_map/all_gather | solution.py:37
  93.2 4.1 %fusion = (f32[8,2,128]{2,1,0:T(2,128)S(1)}, f32[8,1024,128,2]{2,1,3,0:T(8,128)S(1)}) fusion(pred[128,1024]{0,1:T(8,128)(4,1)S(1)} %broadcast_compare_fusion, bf16[1024,8,128,1]{0,2,3,1:T(8,128)(2,1)} %bitcast.66, bf16[128,8,2,128]{3,2,1,0:T(2,128)(2,1)S(1)} %reshape_squeeze.7), kind=kOutput, calls=%fused_computation.1 | convolution fusion | flops 545257472 | bytes 11149312 | tf_op jit(solution)/shard_map/thgd,nhd->hgtn/dot_general | solution.py:16
  97.3 3.4 divide_convert_fusion
  100.8 115.8 %all-gather.8.cloned.1.call-done = bf16[2048,576]{1,0:T(8,128)(2,1)} async-done(((bf16[32,576]{1,0:T(8,128)(2,1)}), bf16[2048,576]{1,0:T(8,128)(2,1)}) %all-gather.8.cloned.1.call-update) | async-done | bytes 2359312 | tf_op jit(solution)/shard_map/all_gather | solution.py:34
  216.6 88.3 %all-gather.6.cloned.1.call-done = bf16[1,1024,2048]{1,2,0:T(8,128)(2,1)} async-done(((bf16[1,128,2048]{1,2,0:T(8,128)(2,1)}), bf16[1,1024,2048]{1,2,0:T(8,128)(2,1)}) %all-gather.6.cloned.1.call-update) | async-done | bytes 4194320 | tf_op jit(solution)/shard_map/all_gather | solution.py:52
  304.9 5.7 %fusion.14 = bf16[72,8,8,128]{3,2,1,0:T(8,128)(2,1)S(1)} fusion(bf16[2048,576]{1,0:T(8,128)(2,1)} %all-gather.8.cloned.1.call-done, bf16[1,1024,2048]{1,2,0:T(8,128)(2,1)} %all-gather.6.cloned.1.call-done), kind=kOutput, calls=%fused_computation.14 | convolution fusion | flops 2416508928 | bytes 7733248 | tf_op jit(solution)/shard_map/dot_general | solution.py:51
  310.6 1.2 copy.40
  311.8 3.6 %all-to-all-start.1 = ((bf16[8,128,576]{1,2,0:T(8,128)(2,1)}), bf16[8,128,576]{1,2,0:T(8,128)(2,1)S(1)}, u32[]{:S(2)}, u32[]{:S(2)}) async-start(bf16[8,128,576]{1,2,0:T(8,128)(2,1)} %bitcast.59), calls=%async_computation.1 | async-start | bytes 2359296 | tf_op jit(solution)/shard_map/all_to_all | solution.py:56
  315.4 0.7 copy.20
  316.1 16.1 %all-to-all-done.1 = bf16[8,128,576]{1,2,0:T(8,128)(2,1)S(1)} async-done(((bf16[8,128,576]{1,2,0:T(8,128)(2,1)}), bf16[8,128,576]{1,2,0:T(8,128)(2,1)S(1)}, u32[]{:S(2)}, u32[]{:S(2)}) %all-to-all-start.1) | async-done | bytes 1179680 | tf_op jit(solution)/shard_map/all_to_all | solution.py:56
  332.3 0.6 multiply_reduce_fusion
  332.9 0.2 convert_element_type.47
  333.1 2.0 fusion.9
  335.1 1.4 copy.28
  (15 shorter events, 0.1 us)
Async XLA Ops:
  6.5 86.6 %all-gather.4.cloned.1.call-start = ((), (), s32[]{:S(2)}) async-start(), calls=%async_computation.2 | async-start | bytes 2359296 | tf_op jit(solution)/shard_map/all_gather | solution.py:37
  8.4 208.2 %all-gather.8.cloned.1.call-start = ((), (), s32[]{:S(2)}) async-start(), calls=%async_computation.4 | async-start | bytes 2662400 | tf_op jit(solution)/shard_map/all_gather | solution.py:34
  11.8 7.1 %copy-start.1 = (bf16[1,128,2048]{2,1,0:T(8,128)(2,1)S(1)}, bf16[1,128,2048]{2,1,0:T(8,128)(2,1)}, u32[]{:S(2)}) copy-start(bf16[1,128,2048]{2,1,0:T(8,128)(2,1)} %param.8) | copy-start | bytes 1572868
  11.8 7.5 %copy-start.3 = (s32[1,128]{1,0:T(1,128)S(1)}, s32[1,128]{1,0:T(1,128)}, u32[]{:S(2)}) copy-start(s32[1,128]{1,0:T(1,128)} %param.11) | copy-start | bytes 1540
  11.8 49.7 %all-to-all-start = ((bf16[8,1,128,1024]{2,3,1,0:T(8,128)(2,1)}), bf16[8,1,128,1024]{2,3,1,0:T(8,128)(2,1)S(1)}, u32[]{:S(2)}, u32[]{:S(2)}) async-start(bf16[8,1,128,1024]{2,3,1,0:T(8,128)(2,1)} %stack.2), calls=%async_computation | async-start | bytes 4194304 | tf_op jit(solution)/shard_map/all_to_all | solution.py:39
  18.9 286.0 %all-gather.6.cloned.1.call-start = ((), (), s32[]{:S(2)}) async-start(), calls=%async_computation.3 | async-start | bytes 4718592 | tf_op jit(solution)/shard_map/all_gather | solution.py:52
  310.6 4.8 %copy-start = (bf16[1,128,4608]{2,1,0:T(8,128)(2,1)S(1)}, bf16[1,128,4608]{2,1,0:T(8,128)(2,1)}, u32[]{:S(2)}) copy-start(bf16[1,128,4608]{2,1,0:T(8,128)(2,1)} %param.7) | copy-start | bytes 3538948
  311.8 20.5 %all-to-all-start.1 = ((bf16[8,128,576]{1,2,0:T(8,128)(2,1)}), bf16[8,128,576]{1,2,0:T(8,128)(2,1)S(1)}, u32[]{:S(2)}, u32[]{:S(2)}) async-start(bf16[8,128,576]{1,2,0:T(8,128)(2,1)} %bitcast.59), calls=%async_computation.1 | async-start | bytes 2359296 | tf_op jit(solution)/shard_map/all_to_all | solution.py:56
  316.1 16.9 %copy-start.2 = (f32[4608]{0:T(1024)S(1)}, f32[4608]{0:T(1024)}, u32[]{:S(2)}) copy-start(f32[4608]{0:T(1024)} %param.12) | copy-start | bytes 55300
Sparse Core Ops, SparseCore 0:
  10.4 82.7 all-gather.3
  95.3 121.2 all-gather.7
  219.6 85.1 all-gather.5
